TPU v7x, 256 devices: a whole 4x4x8 slice. The times are simulated.
256 devices in a mesh: tile: 32 (over z, x), col: 8 (over y, core).
Axes of the slice: x: 4, y: 4, z: 8, core: 2. Of those that a mesh axis runs over, the one named last changes fastest.
Arguments:
- section_image: bfloat16 [12288, 8192], P('tile', 'col'), may hold values from -6 to 6
- peak_offsets: int32 [2, 64, 64], P(None, None, 'col'), may hold values from -8 to 8
Outputs:
- mesh_shift: float32 [2, 96, 64], P(None, 'tile', 'col')
All inputs are finite; a program needn't handle non-finite values.
Results may differ from a plain program's by a relative error of at most 0.00075.
Values may be sent and summed in bfloat16 or wider, within the bound.
A program may use at most 64 MiB of HBM per device.

v0:
```python
import math

import jax
import jax.numpy as jnp
from jax import lax
from jax.sharding import PartitionSpec as P

SECTIONS = 3
PATCH = 128
ITERS = 8


def from_behind(shard, axis, by):
    count = lax.axis_size(axis)
    pairs = [(i, i + by) for i in range(count) if 0 <= i + by < count]
    return lax.ppermute(shard, axis, pairs)


def with_halo(block, sides, width):
    for axis, dim in sides:
        count = lax.axis_size(axis)
        forward = [(i, i + 1) for i in range(count - 1)]
        backward = [(target, source) for source, target in forward]
        low = lax.ppermute(
            lax.slice_in_dim(block, block.shape[dim] - width, None, axis=dim), axis, forward
        )
        high = lax.ppermute(lax.slice_in_dim(block, 0, width, axis=dim), axis, backward)
        block = jnp.concatenate([low, block, high], axis=dim)
    return block


def dft_tables(length):
    counter = jnp.arange(length, dtype=jnp.int32)
    product = jnp.mod(counter[:, None] * counter[None, :], length)
    phase = product.astype(jnp.float32) * (2.0 * math.pi / length)
    return (jnp.cos(phase).astype(jnp.bfloat16), jnp.sin(phase).astype(jnp.bfloat16))


def spectrum(blocks, cosine, sine):
    row_cos = jnp.einsum(
        "ky,nymx->nkmx", cosine, blocks, preferred_element_type=jnp.float32
    ).astype(jnp.bfloat16)
    row_sin = jnp.einsum("ky,nymx->nkmx", sine, blocks, preferred_element_type=jnp.float32).astype(
        jnp.bfloat16
    )
    spec_real = (
        jnp.einsum("nkmx,xl->nkml", row_cos, cosine, preferred_element_type=jnp.float32)
        - jnp.einsum("nkmx,xl->nkml", row_sin, sine, preferred_element_type=jnp.float32)
    ).astype(jnp.bfloat16)
    spec_imag = (
        jnp.einsum("nkmx,xl->nkml", row_cos, sine, preferred_element_type=jnp.float32)
        + jnp.einsum("nkmx,xl->nkml", row_sin, cosine, preferred_element_type=jnp.float32)
    ).astype(jnp.bfloat16)
    return (spec_real, spec_imag)


def correlate(left_real, left_imag, right_real, right_imag, cosine, sine):
    lr = left_real.astype(jnp.float32)
    li = left_imag.astype(jnp.float32)
    rr = right_real.astype(jnp.float32)
    ri = right_imag.astype(jnp.float32)
    cross_real = (lr * rr + li * ri).astype(jnp.bfloat16)
    cross_imag = (li * rr - lr * ri).astype(jnp.bfloat16)
    mixed_real = (
        jnp.einsum("pk,nkml->npml", cosine, cross_real, preferred_element_type=jnp.float32)
        - jnp.einsum("pk,nkml->npml", sine, cross_imag, preferred_element_type=jnp.float32)
    ).astype(jnp.bfloat16)
    mixed_imag = (
        jnp.einsum("pk,nkml->npml", sine, cross_real, preferred_element_type=jnp.float32)
        + jnp.einsum("pk,nkml->npml", cosine, cross_imag, preferred_element_type=jnp.float32)
    ).astype(jnp.bfloat16)
    length = cosine.shape[0]
    scale_back = 1.0 / float(length * length * length)
    return (
        jnp.einsum("npml,lq->npmq", mixed_real, cosine, preferred_element_type=jnp.float32)
        - jnp.einsum("npml,lq->npmq", mixed_imag, sine, preferred_element_type=jnp.float32)
    ) * scale_back


def flow_of(correlation, peak_row, peak_col):
    count, length, width, _ = correlation.shape
    offsets = jnp.arange(3, dtype=jnp.int32) - 1
    row_pick = jnp.mod(peak_row[:, None, :, None] + offsets[None, :, None, None], length)
    row_pick = jnp.broadcast_to(row_pick, (count, 3, width, length))
    picked = jnp.take_along_axis(correlation, row_pick, axis=1)
    col_pick = jnp.mod(peak_col[:, None, :, None] + offsets[None, None, None, :], length)
    col_pick = jnp.broadcast_to(col_pick, (count, 3, width, 3))
    window = jnp.take_along_axis(picked, col_pick, axis=3)
    window_min = jnp.min(window, axis=(1, 3), keepdims=True)
    weight = window - window_min + 0.5
    weight_sum = jnp.sum(weight, axis=(1, 3))
    steps_f = offsets.astype(jnp.float32)
    flow_row = (
        peak_row.astype(jnp.float32)
        + jnp.sum(weight * steps_f[None, :, None, None], axis=(1, 3)) / weight_sum
    )
    flow_col = (
        peak_col.astype(jnp.float32)
        + jnp.sum(weight * steps_f[None, None, None, :], axis=(1, 3)) / weight_sum
    )
    return jnp.stack([flow_row, flow_col])


def shards(section_image, peak_offsets):
    patch_rows = section_image.shape[0] // PATCH
    patch_cols = section_image.shape[1] // PATCH
    sec_rows = patch_rows * lax.axis_size("tile") // SECTIONS
    far_hops = sec_rows // patch_rows
    remain = sec_rows % patch_rows
    pair_rows = (SECTIONS - 1) * sec_rows
    grid_cols = patch_cols * lax.axis_size("col")
    row_start = lax.axis_index("tile") * patch_rows
    col_start = lax.axis_index("col") * patch_cols
    cosine, sine = dft_tables(PATCH)
    blocks = section_image.reshape(patch_rows, PATCH, patch_cols, PATCH)
    upper_part = from_behind(blocks[remain:], "tile", -far_hops)
    lower_part = from_behind(blocks[:remain], "tile", -(far_hops + 1))
    own_real, own_imag = spectrum(blocks, cosine, sine)
    partner = jnp.concatenate([upper_part, lower_part], axis=0)
    next_real, next_imag = spectrum(partner, cosine, sine)
    correlation = correlate(own_real, own_imag, next_real, next_imag, cosine, sine)
    padded_peaks = jnp.pad(peak_offsets, ((0, 0), (0, patch_rows), (0, 0)))
    local_peaks = lax.dynamic_slice_in_dim(padded_peaks, row_start, patch_rows, 1)
    row_number = row_start + jnp.arange(patch_rows, dtype=jnp.int32)
    pair_ok = (row_number < pair_rows)[None, :, None]
    flow_field = jnp.where(pair_ok, flow_of(correlation, local_peaks[0], local_peaks[1]), 0.0)
    row_in_section = jnp.mod(row_number, sec_rows)
    up_ok = (row_in_section != 0)[None, :, None]
    down_ok = (row_in_section != sec_rows - 1)[None, :, None]
    col_number = col_start + jnp.arange(patch_cols, dtype=jnp.int32)
    left_ok = (col_number != 0)[None, None, :]
    right_ok = (col_number != grid_cols - 1)[None, None, :]
    mesh_shift = jnp.zeros((2, patch_rows, patch_cols), jnp.float32)
    for sweep in range(ITERS):
        padded = with_halo(mesh_shift, (("tile", 1), ("col", 2)), 1)
        spring_pull = jnp.where(up_ok, mesh_shift - padded[:, :-2, 1:-1], 0.0)
        spring_pull = spring_pull + jnp.where(down_ok, mesh_shift - padded[:, 2:, 1:-1], 0.0)
        spring_pull = spring_pull + jnp.where(left_ok, mesh_shift - padded[:, 1:-1, :-2], 0.0)
        spring_pull = spring_pull + jnp.where(right_ok, mesh_shift - padded[:, 1:-1, 2:], 0.0)
        ahead_upper = from_behind(mesh_shift[:, remain:], "tile", -far_hops)
        ahead_lower = from_behind(mesh_shift[:, :remain], "tile", -(far_hops + 1))
        ahead_rows = jnp.concatenate([ahead_upper, ahead_lower], axis=1)
        pair_error = jnp.where(pair_ok, ahead_rows - mesh_shift - flow_field, 0.0)
        behind_upper = from_behind(pair_error[:, patch_rows - remain :], "tile", far_hops + 1)
        behind_lower = from_behind(pair_error[:, : patch_rows - remain], "tile", far_hops)
        behind_error = jnp.concatenate([behind_upper, behind_lower], axis=1)
        mesh_shift = mesh_shift - 0.12 * (1.0 * spring_pull - pair_error + behind_error)
    return mesh_shift


def solution(mesh):
    return jax.shard_map(
        shards,
        mesh=mesh,
        in_specs=(P("tile", "col"), P(None, None, "col")),
        out_specs=P(None, "tile", "col"),
        check_vma=False,
    )
```

profile of v0, /device:TPU:1, one launch (start us, length us, event | category | flops | bytes accessed | tf_op | source)
XLA Modules:
  0.0 432.7 jit_solution(1366489765414313892)
XLA Ops:
  3.2 5.2 %collective-permute-start = (f32[2,1,8]{2,1,0:T(1,128)}, f32[2,1,8]{2,1,0:T(1,128)}, u32[]{:S(2)}, u32[]{:S(2)}) collective-permute-start(f32[2,1,8]{2,1,0:T(1,128)} %broadcast.281), channel_id=1, source_target_pairs={{0,8},{8,16},{16,24},{24,32},{32,40},{40,48},{48,56},{56,64},{64,7... | collective-permute-start | bytes 200 | tf_op jit(solution)/shard_map/ppermute | solution.py:24
  18.4 2.0 add_convert_fusion.2
  25.5 4.6 %collective-permute-start.2 = (f32[2,5,1]{2,1,0:T(8,128)}, f32[2,5,1]{2,1,0:T(8,128)}, u32[]{:S(2)}, u32[]{:S(2)}) collective-permute-start(f32[2,5,1]{2,1,0:T(8,128)} %get-tuple-element.30), channel_id=1, source_target_pairs={{0,1},{1,2},{2,3},{3,4},{4,5},{5,6},{6,7},{8,9},{9,10},{10,11},{11... | collective-permute-start | bytes 128 | tf_op jit(solution)/shard_map/ppermute | solution.py:24
  30.0 16.2 %collective-permute-done.6 = bf16[1,128,8,128]{1,3,2,0:T(8,128)(2,1)S(1)} collective-permute-done((bf16[1,128,8,128]{1,3,2,0:T(8,128)(2,1)S(1)}, bf16[1,128,8,128]{1,3,2,0:T(8,128)(2,1)S(1)}, u32[]{:S(2)}, u32[]{:S(2)}) %collective-permute-start.6) | collective-permute-done | bytes 262176 | tf_op jit(solution)/shard_map/ppermute | solution.py:16
  46.3 4.1 collective-permute-start.3
  60.3 2.0 fusion.9
  62.3 2.7 subtract_multiply_fusion
  65.0 88.4 %gather_fusion = f32[9216]{0:T(1024)S(1)} fusion(f32[3,128,8,128]{3,1,2,0:T(8,128)S(1)} %subtract_multiply_fusion, s32[9216]{0:T(1024)S(1)} %bitcast.82), kind=kCustom, calls=%fused_computation | custom fusion | bytes 221184 | tf_op jit(solution)/shard_map/jit(take_along_axis)/gather | solution.py:85
  153.5 3.5 gather_fusion.1
  158.2 32.2 %collective-permute-start.9 = (f32[2,1,8]{2,1,0:T(1,128)S(1)}, f32[2,1,8]{2,1,0:T(1,128)S(1)}, u32[]{:S(2)}, u32[]{:S(2)}) collective-permute-start(f32[2,1,8]{2,1,0:T(1,128)S(1)} %slice.418), channel_id=1, source_target_pairs={{0,80},{8,88},{16,96},{24,104},{32,112},{40,120},{48,128},{56,136}... | collective-permute-start | bytes 200 | tf_op jit(solution)/shard_map/ppermute | solution.py:16
  198.5 2.0 collective-permute-done.11
  200.6 4.8 %collective-permute-start.12 = (f32[2,5,1]{2,1,0:T(8,128)S(1)}, f32[2,5,1]{2,1,0:T(8,128)S(1)}, u32[]{:S(2)}, u32[]{:S(2)}) collective-permute-start(f32[2,5,1]{2,1,0:T(8,128)S(1)} %get-tuple-element.28), channel_id=1, source_target_pairs={{0,1},{1,2},{2,3},{3,4},{4,5},{5,6},{6,7},{8,9},{9,10},{10,11},{11... | collective-permute-start | bytes 128 | tf_op jit(solution)/shard_map/ppermute | solution.py:24
  205.4 1.9 collective-permute-start.13
  208.3 8.7 %collective-permute-start.17 = (f32[2,1,8]{2,1,0:T(1,128)S(1)}, f32[2,1,8]{2,1,0:T(1,128)S(1)}, u32[]{:S(2)}, u32[]{:S(2)}) collective-permute-start(f32[2,1,8]{2,1,0:T(1,128)S(1)} %slice.425), channel_id=1, source_target_pairs={{0,80},{8,88},{16,96},{24,104},{32,112},{40,120},{48,128},{56,136}... | collective-permute-start | bytes 200 | tf_op jit(solution)/shard_map/ppermute | solution.py:16
  217.1 7.6 %collective-permute-start.16 = (f32[2,2,8]{2,1,0:T(2,128)S(1)}, f32[2,2,8]{2,1,0:T(2,128)S(1)}, u32[]{:S(2)}, u32[]{:S(2)}) collective-permute-start(f32[2,2,8]{2,1,0:T(2,128)S(1)} %slice.424), channel_id=1, source_target_pairs={{0,88},{8,96},{16,104},{24,112},{32,120},{40,128},{48,136},{56,144... | collective-permute-start | bytes 392 | tf_op jit(solution)/shard_map/ppermute | solution.py:16
  226.8 2.0 collective-permute-start.18
  233.2 6.2 %collective-permute-start.20 = (f32[2,5,1]{2,1,0:T(8,128)S(1)}, f32[2,5,1]{2,1,0:T(8,128)S(1)}, u32[]{:S(2)}, u32[]{:S(2)}) collective-permute-start(f32[2,5,1]{2,1,0:T(8,128)S(1)} %get-tuple-element.26), channel_id=1, source_target_pairs={{0,1},{1,2},{2,3},{3,4},{4,5},{5,6},{6,7},{8,9},{9,10},{10,11},{11... | collective-permute-start | bytes 128 | tf_op jit(solution)/shard_map/ppermute | solution.py:24
  239.4 1.9 collective-permute-start.21
  241.5 8.6 %collective-permute-start.25 = (f32[2,1,8]{2,1,0:T(1,128)S(1)}, f32[2,1,8]{2,1,0:T(1,128)S(1)}, u32[]{:S(2)}, u32[]{:S(2)}) collective-permute-start(f32[2,1,8]{2,1,0:T(1,128)S(1)} %slice.432), channel_id=1, source_target_pairs={{0,80},{8,88},{16,96},{24,104},{32,112},{40,120},{48,128},{56,136}... | collective-permute-start | bytes 200 | tf_op jit(solution)/shard_map/ppermute | solution.py:16
  250.1 7.7 %collective-permute-start.24 = (f32[2,2,8]{2,1,0:T(2,128)S(1)}, f32[2,2,8]{2,1,0:T(2,128)S(1)}, u32[]{:S(2)}, u32[]{:S(2)}) collective-permute-start(f32[2,2,8]{2,1,0:T(2,128)S(1)} %slice.431), channel_id=1, source_target_pairs={{0,88},{8,96},{16,104},{24,112},{32,120},{40,128},{48,136},{56,144... | collective-permute-start | bytes 392 | tf_op jit(solution)/shard_map/ppermute | solution.py:16
  260.0 1.9 collective-permute-start.26
  264.5 2.3 collective-permute-done.27
  266.9 5.9 %collective-permute-start.28 = (f32[2,5,1]{2,1,0:T(8,128)S(1)}, f32[2,5,1]{2,1,0:T(8,128)S(1)}, u32[]{:S(2)}, u32[]{:S(2)}) collective-permute-start(f32[2,5,1]{2,1,0:T(8,128)S(1)} %get-tuple-element.24), channel_id=1, source_target_pairs={{0,1},{1,2},{2,3},{3,4},{4,5},{5,6},{6,7},{8,9},{9,10},{10,11},{11... | collective-permute-start | bytes 128 | tf_op jit(solution)/shard_map/ppermute | solution.py:24
  272.8 1.9 collective-permute-start.29
  275.1 9.4 %collective-permute-start.33 = (f32[2,1,8]{2,1,0:T(1,128)S(1)}, f32[2,1,8]{2,1,0:T(1,128)S(1)}, u32[]{:S(2)}, u32[]{:S(2)}) collective-permute-start(f32[2,1,8]{2,1,0:T(1,128)S(1)} %slice.439), channel_id=1, source_target_pairs={{0,80},{8,88},{16,96},{24,104},{32,112},{40,120},{48,128},{56,136}... | collective-permute-start | bytes 200 | tf_op jit(solution)/shard_map/ppermute | solution.py:16
  284.5 8.0 %collective-permute-start.32 = (f32[2,2,8]{2,1,0:T(2,128)S(1)}, f32[2,2,8]{2,1,0:T(2,128)S(1)}, u32[]{:S(2)}, u32[]{:S(2)}) collective-permute-start(f32[2,2,8]{2,1,0:T(2,128)S(1)} %slice.438), channel_id=1, source_target_pairs={{0,88},{8,96},{16,104},{24,112},{32,120},{40,128},{48,136},{56,144... | collective-permute-start | bytes 392 | tf_op jit(solution)/shard_map/ppermute | solution.py:16
  294.7 1.9 collective-permute-start.34
  299.2 2.3 collective-permute-done.35
  301.6 5.9 %collective-permute-start.36 = (f32[2,5,1]{2,1,0:T(8,128)S(1)}, f32[2,5,1]{2,1,0:T(8,128)S(1)}, u32[]{:S(2)}, u32[]{:S(2)}) collective-permute-start(f32[2,5,1]{2,1,0:T(8,128)S(1)} %get-tuple-element.22), channel_id=1, source_target_pairs={{0,1},{1,2},{2,3},{3,4},{4,5},{5,6},{6,7},{8,9},{9,10},{10,11},{11... | collective-permute-start | bytes 128 | tf_op jit(solution)/shard_map/ppermute | solution.py:24
  307.5 1.9 collective-permute-start.37
  309.8 9.4 %collective-permute-start.41 = (f32[2,1,8]{2,1,0:T(1,128)S(1)}, f32[2,1,8]{2,1,0:T(1,128)S(1)}, u32[]{:S(2)}, u32[]{:S(2)}) collective-permute-start(f32[2,1,8]{2,1,0:T(1,128)S(1)} %slice.446), channel_id=1, source_target_pairs={{0,80},{8,88},{16,96},{24,104},{32,112},{40,120},{48,128},{56,136}... | collective-permute-start | bytes 200 | tf_op jit(solution)/shard_map/ppermute | solution.py:16
  319.2 8.0 %collective-permute-start.40 = (f32[2,2,8]{2,1,0:T(2,128)S(1)}, f32[2,2,8]{2,1,0:T(2,128)S(1)}, u32[]{:S(2)}, u32[]{:S(2)}) collective-permute-start(f32[2,2,8]{2,1,0:T(2,128)S(1)} %slice.445), channel_id=1, source_target_pairs={{0,88},{8,96},{16,104},{24,112},{32,120},{40,128},{48,136},{56,144... | collective-permute-start | bytes 392 | tf_op jit(solution)/shard_map/ppermute | solution.py:16
  329.4 1.9 collective-permute-start.42
  333.9 2.3 collective-permute-done.43
  336.2 5.9 %collective-permute-start.44 = (f32[2,5,1]{2,1,0:T(8,128)S(1)}, f32[2,5,1]{2,1,0:T(8,128)S(1)}, u32[]{:S(2)}, u32[]{:S(2)}) collective-permute-start(f32[2,5,1]{2,1,0:T(8,128)S(1)} %get-tuple-element.20), channel_id=1, source_target_pairs={{0,1},{1,2},{2,3},{3,4},{4,5},{5,6},{6,7},{8,9},{9,10},{10,11},{11... | collective-permute-start | bytes 128 | tf_op jit(solution)/shard_map/ppermute | solution.py:24
  342.2 1.9 collective-permute-start.45
  344.5 9.4 %collective-permute-start.49 = (f32[2,1,8]{2,1,0:T(1,128)S(1)}, f32[2,1,8]{2,1,0:T(1,128)S(1)}, u32[]{:S(2)}, u32[]{:S(2)}) collective-permute-start(f32[2,1,8]{2,1,0:T(1,128)S(1)} %slice.453), channel_id=1, source_target_pairs={{0,80},{8,88},{16,96},{24,104},{32,112},{40,120},{48,128},{56,136}... | collective-permute-start | bytes 200 | tf_op jit(solution)/shard_map/ppermute | solution.py:16
  353.9 8.0 %collective-permute-start.48 = (f32[2,2,8]{2,1,0:T(2,128)S(1)}, f32[2,2,8]{2,1,0:T(2,128)S(1)}, u32[]{:S(2)}, u32[]{:S(2)}) collective-permute-start(f32[2,2,8]{2,1,0:T(2,128)S(1)} %slice.452), channel_id=1, source_target_pairs={{0,88},{8,96},{16,104},{24,112},{32,120},{40,128},{48,136},{56,144... | collective-permute-start | bytes 392 | tf_op jit(solution)/shard_map/ppermute | solution.py:16
  368.6 2.3 collective-permute-done.51
  370.9 5.9 %collective-permute-start.52 = (f32[2,5,1]{2,1,0:T(8,128)S(1)}, f32[2,5,1]{2,1,0:T(8,128)S(1)}, u32[]{:S(2)}, u32[]{:S(2)}) collective-permute-start(f32[2,5,1]{2,1,0:T(8,128)S(1)} %get-tuple-element.18), channel_id=1, source_target_pairs={{0,1},{1,2},{2,3},{3,4},{4,5},{5,6},{6,7},{8,9},{9,10},{10,11},{11... | collective-permute-start | bytes 128 | tf_op jit(solution)/shard_map/ppermute | solution.py:24
  376.8 1.9 collective-permute-start.53
  379.2 9.4 %collective-permute-start.57 = (f32[2,1,8]{2,1,0:T(1,128)S(1)}, f32[2,1,8]{2,1,0:T(1,128)S(1)}, u32[]{:S(2)}, u32[]{:S(2)}) collective-permute-start(f32[2,1,8]{2,1,0:T(1,128)S(1)} %slice.460), channel_id=1, source_target_pairs={{0,80},{8,88},{16,96},{24,104},{32,112},{40,120},{48,128},{56,136}... | collective-permute-start | bytes 200 | tf_op jit(solution)/shard_map/ppermute | solution.py:16
  388.6 8.0 %collective-permute-start.56 = (f32[2,2,8]{2,1,0:T(2,128)S(1)}, f32[2,2,8]{2,1,0:T(2,128)S(1)}, u32[]{:S(2)}, u32[]{:S(2)}) collective-permute-start(f32[2,2,8]{2,1,0:T(2,128)S(1)} %slice.459), channel_id=1, source_target_pairs={{0,88},{8,96},{16,104},{24,112},{32,120},{40,128},{48,136},{56,144... | collective-permute-start | bytes 392 | tf_op jit(solution)/shard_map/ppermute | solution.py:16
  403.3 2.3 collective-permute-done.59
  405.6 5.9 %collective-permute-start.60 = (f32[2,5,1]{2,1,0:T(8,128)S(1)}, f32[2,5,1]{2,1,0:T(8,128)S(1)}, u32[]{:S(2)}, u32[]{:S(2)}) collective-permute-start(f32[2,5,1]{2,1,0:T(8,128)S(1)} %get-tuple-element.16), channel_id=1, source_target_pairs={{0,1},{1,2},{2,3},{3,4},{4,5},{5,6},{6,7},{8,9},{9,10},{10,11},{11... | collective-permute-start | bytes 128 | tf_op jit(solution)/shard_map/ppermute | solution.py:24
  411.5 1.9 collective-permute-start.61
  413.8 9.4 %collective-permute-start.65 = (f32[2,1,8]{2,1,0:T(1,128)S(1)}, f32[2,1,8]{2,1,0:T(1,128)S(1)}, u32[]{:S(2)}, u32[]{:S(2)}) collective-permute-start(f32[2,1,8]{2,1,0:T(1,128)S(1)} %slice.467), channel_id=1, source_target_pairs={{0,80},{8,88},{16,96},{24,104},{32,112},{40,120},{48,128},{56,136}... | collective-permute-start | bytes 200 | tf_op jit(solution)/shard_map/ppermute | solution.py:16
  423.2 8.0 %collective-permute-start.64 = (f32[2,2,8]{2,1,0:T(2,128)S(1)}, f32[2,2,8]{2,1,0:T(2,128)S(1)}, u32[]{:S(2)}, u32[]{:S(2)}) collective-permute-start(f32[2,2,8]{2,1,0:T(2,128)S(1)} %slice.466), channel_id=1, source_target_pairs={{0,88},{8,96},{16,104},{24,112},{32,120},{40,128},{48,136},{56,144... | collective-permute-start | bytes 392 | tf_op jit(solution)/shard_map/ppermute | solution.py:16
  (203 shorter events, 75.8 us)
Async XLA Ops:
  0.6 156.8 %collective-permute-start.4 = (f32[2,1,8]{2,1,0:T(1,128)}, f32[2,1,8]{2,1,0:T(1,128)}, u32[]{:S(2)}, u32[]{:S(2)}) collective-permute-start(f32[2,1,8]{2,1,0:T(1,128)} %broadcast.281), channel_id=1, source_target_pairs={{80,0},{88,8},{96,16},{104,24},{112,32},{120,40},{128,48},{136,56}... | collective-permute-start | bytes 200 | tf_op jit(solution)/shard_map/ppermute | solution.py:16
  1.9 20.9 %collective-permute-start.1 = (f32[2,1,8]{2,1,0:T(1,128)}, f32[2,1,8]{2,1,0:T(1,128)}, u32[]{:S(2)}, u32[]{:S(2)}) collective-permute-start(f32[2,1,8]{2,1,0:T(1,128)} %broadcast.281), channel_id=1, source_target_pairs={{8,0},{16,8},{24,16},{32,24},{40,32},{48,40},{56,48},{64,56},{72,6... | collective-permute-start | bytes 200 | tf_op jit(solution)/shard_map/ppermute | solution.py:27
  3.2 20.9 %collective-permute-start = (f32[2,1,8]{2,1,0:T(1,128)}, f32[2,1,8]{2,1,0:T(1,128)}, u32[]{:S(2)}, u32[]{:S(2)}) collective-permute-start(f32[2,1,8]{2,1,0:T(1,128)} %broadcast.281), channel_id=1, source_target_pairs={{0,8},{8,16},{16,24},{24,32},{32,40},{40,48},{48,56},{56,64},{64,7... | collective-permute-start | bytes 200 | tf_op jit(solution)/shard_map/ppermute | solution.py:24
  8.9 148.5 %collective-permute-start.5 = (f32[2,2,8]{2,1,0:T(2,128)}, f32[2,2,8]{2,1,0:T(2,128)S(1)}, u32[]{:S(2)}, u32[]{:S(2)}) collective-permute-start(f32[2,2,8]{2,1,0:T(2,128)} %slice.321), channel_id=1, source_target_pairs={{88,0},{96,8},{104,16},{112,24},{120,32},{128,40},{136,48},{144,56... | collective-permute-start | bytes 392 | tf_op jit(solution)/shard_map/ppermute | solution.py:16
  12.6 39.6 %collective-permute-start.7 = (bf16[2,128,8,128]{1,3,2,0:T(8,128)(2,1)}, bf16[2,128,8,128]{1,3,2,0:T(8,128)(2,1)}, u32[]{:S(2)}, u32[]{:S(2)}) collective-permute-start(bf16[2,128,8,128]{1,3,2,0:T(8,128)(2,1)} %copy.16), channel_id=1, source_target_pairs={{88,0},{96,8},{104,16},{112,24},{120,32},{128,40},{136,48},{144,56... | collective-permute-start | bytes 1572872 | tf_op jit(solution)/shard_map/ppermute | solution.py:16
  22.8 23.5 %collective-permute-start.6 = (bf16[1,128,8,128]{1,3,2,0:T(8,128)(2,1)S(1)}, bf16[1,128,8,128]{1,3,2,0:T(8,128)(2,1)S(1)}, u32[]{:S(2)}, u32[]{:S(2)}) collective-permute-start(bf16[1,128,8,128]{1,3,2,0:T(8,128)(2,1)S(1)} %bitcast.87), channel_id=1, source_target_pairs={{80,0},{88,8},{96,16},{104,24},{112,32},{120,40},{128,48},{136,56}... | collective-permute-start | bytes 786440 | tf_op jit(solution)/shard_map/ppermute | solution.py:16
  25.5 166.2 %collective-permute-start.2 = (f32[2,5,1]{2,1,0:T(8,128)}, f32[2,5,1]{2,1,0:T(8,128)}, u32[]{:S(2)}, u32[]{:S(2)}) collective-permute-start(f32[2,5,1]{2,1,0:T(8,128)} %get-tuple-element.30), channel_id=1, source_target_pairs={{0,1},{1,2},{2,3},{3,4},{4,5},{5,6},{6,7},{8,9},{9,10},{10,11},{11... | collective-permute-start | bytes 128 | tf_op jit(solution)/shard_map/ppermute | solution.py:24
  46.3 145.4 %collective-permute-start.3 = (f32[2,5,1]{2,1,0:T(8,128)}, f32[2,5,1]{2,1,0:T(8,128)}, u32[]{:S(2)}, u32[]{:S(2)}) collective-permute-start(f32[2,5,1]{2,1,0:T(8,128)} %get-tuple-element.31), channel_id=1, source_target_pairs={{1,0},{2,1},{3,2},{4,3},{5,4},{6,5},{7,6},{9,8},{10,9},{11,10},{12... | collective-permute-start | bytes 128 | tf_op jit(solution)/shard_map/ppermute | solution.py:27
  158.2 33.5 %collective-permute-start.9 = (f32[2,1,8]{2,1,0:T(1,128)S(1)}, f32[2,1,8]{2,1,0:T(1,128)S(1)}, u32[]{:S(2)}, u32[]{:S(2)}) collective-permute-start(f32[2,1,8]{2,1,0:T(1,128)S(1)} %slice.418), channel_id=1, source_target_pairs={{0,80},{8,88},{16,96},{24,104},{32,112},{40,120},{48,128},{56,136}... | collective-permute-start | bytes 200 | tf_op jit(solution)/shard_map/ppermute | solution.py:16
  193.3 14.0 %collective-permute-start.14 = (f32[2,1,8]{2,1,0:T(1,128)S(1)}, f32[2,1,8]{2,1,0:T(1,128)S(1)}, u32[]{:S(2)}, u32[]{:S(2)}) collective-permute-start(f32[2,1,8]{2,1,0:T(1,128)S(1)} %get-tuple-element.45), channel_id=1, source_target_pairs={{80,0},{88,8},{96,16},{104,24},{112,32},{120,40},{128,48},{136,56}... | collective-permute-start | bytes 200 | tf_op jit(solution)/shard_map/ppermute | solution.py:16
  197.2 11.0 %collective-permute-start.15 = (f32[2,2,8]{2,1,0:T(2,128)S(1)}, f32[2,2,8]{2,1,0:T(2,128)S(1)}, u32[]{:S(2)}, u32[]{:S(2)}) collective-permute-start(f32[2,2,8]{2,1,0:T(2,128)S(1)} %slice.423), channel_id=1, source_target_pairs={{88,0},{96,8},{104,16},{112,24},{120,32},{128,40},{136,48},{144,56... | collective-permute-start | bytes 392 | tf_op jit(solution)/shard_map/ppermute | solution.py:16
  200.6 24.1 %collective-permute-start.12 = (f32[2,5,1]{2,1,0:T(8,128)S(1)}, f32[2,5,1]{2,1,0:T(8,128)S(1)}, u32[]{:S(2)}, u32[]{:S(2)}) collective-permute-start(f32[2,5,1]{2,1,0:T(8,128)S(1)} %get-tuple-element.28), channel_id=1, source_target_pairs={{0,1},{1,2},{2,3},{3,4},{4,5},{5,6},{6,7},{8,9},{9,10},{10,11},{11... | collective-permute-start | bytes 128 | tf_op jit(solution)/shard_map/ppermute | solution.py:24
  205.4 19.3 %collective-permute-start.13 = (f32[2,5,1]{2,1,0:T(8,128)S(1)}, f32[2,5,1]{2,1,0:T(8,128)S(1)}, u32[]{:S(2)}, u32[]{:S(2)}) collective-permute-start(f32[2,5,1]{2,1,0:T(8,128)S(1)} %get-tuple-element.29), channel_id=1, source_target_pairs={{1,0},{2,1},{3,2},{4,3},{5,4},{6,5},{7,6},{9,8},{10,9},{11,10},{12... | collective-permute-start | bytes 128 | tf_op jit(solution)/shard_map/ppermute | solution.py:27
  208.3 16.4 %collective-permute-start.17 = (f32[2,1,8]{2,1,0:T(1,128)S(1)}, f32[2,1,8]{2,1,0:T(1,128)S(1)}, u32[]{:S(2)}, u32[]{:S(2)}) collective-permute-start(f32[2,1,8]{2,1,0:T(1,128)S(1)} %slice.425), channel_id=1, source_target_pairs={{0,80},{8,88},{16,96},{24,104},{32,112},{40,120},{48,128},{56,136}... | collective-permute-start | bytes 200 | tf_op jit(solution)/shard_map/ppermute | solution.py:16
  225.5 15.8 %collective-permute-start.22 = (f32[2,1,8]{2,1,0:T(1,128)S(1)}, f32[2,1,8]{2,1,0:T(1,128)S(1)}, u32[]{:S(2)}, u32[]{:S(2)}) collective-permute-start(f32[2,1,8]{2,1,0:T(1,128)S(1)} %get-tuple-element.43), channel_id=1, source_target_pairs={{80,0},{88,8},{96,16},{104,24},{112,32},{120,40},{128,48},{136,56}... | collective-permute-start | bytes 200 | tf_op jit(solution)/shard_map/ppermute | solution.py:16
  230.1 11.3 %collective-permute-start.23 = (f32[2,2,8]{2,1,0:T(2,128)S(1)}, f32[2,2,8]{2,1,0:T(2,128)S(1)}, u32[]{:S(2)}, u32[]{:S(2)}) collective-permute-start(f32[2,2,8]{2,1,0:T(2,128)S(1)} %slice.430), channel_id=1, source_target_pairs={{88,0},{96,8},{104,16},{112,24},{120,32},{128,40},{136,48},{144,56... | collective-permute-start | bytes 392 | tf_op jit(solution)/shard_map/ppermute | solution.py:16
  233.2 24.6 %collective-permute-start.20 = (f32[2,5,1]{2,1,0:T(8,128)S(1)}, f32[2,5,1]{2,1,0:T(8,128)S(1)}, u32[]{:S(2)}, u32[]{:S(2)}) collective-permute-start(f32[2,5,1]{2,1,0:T(8,128)S(1)} %get-tuple-element.26), channel_id=1, source_target_pairs={{0,1},{1,2},{2,3},{3,4},{4,5},{5,6},{6,7},{8,9},{9,10},{10,11},{11... | collective-permute-start | bytes 128 | tf_op jit(solution)/shard_map/ppermute | solution.py:24
  239.4 18.4 %collective-permute-start.21 = (f32[2,5,1]{2,1,0:T(8,128)S(1)}, f32[2,5,1]{2,1,0:T(8,128)S(1)}, u32[]{:S(2)}, u32[]{:S(2)}) collective-permute-start(f32[2,5,1]{2,1,0:T(8,128)S(1)} %get-tuple-element.27), channel_id=1, source_target_pairs={{1,0},{2,1},{3,2},{4,3},{5,4},{6,5},{7,6},{9,8},{10,9},{11,10},{12... | collective-permute-start | bytes 128 | tf_op jit(solution)/shard_map/ppermute | solution.py:27
  241.5 16.4 %collective-permute-start.25 = (f32[2,1,8]{2,1,0:T(1,128)S(1)}, f32[2,1,8]{2,1,0:T(1,128)S(1)}, u32[]{:S(2)}, u32[]{:S(2)}) collective-permute-start(f32[2,1,8]{2,1,0:T(1,128)S(1)} %slice.432), channel_id=1, source_target_pairs={{0,80},{8,88},{16,96},{24,104},{32,112},{40,120},{48,128},{56,136}... | collective-permute-start | bytes 200 | tf_op jit(solution)/shard_map/ppermute | solution.py:16
  258.7 16.0 %collective-permute-start.30 = (f32[2,1,8]{2,1,0:T(1,128)S(1)}, f32[2,1,8]{2,1,0:T(1,128)S(1)}, u32[]{:S(2)}, u32[]{:S(2)}) collective-permute-start(f32[2,1,8]{2,1,0:T(1,128)S(1)} %get-tuple-element.41), channel_id=1, source_target_pairs={{80,0},{88,8},{96,16},{104,24},{112,32},{120,40},{128,48},{136,56}... | collective-permute-start | bytes 200 | tf_op jit(solution)/shard_map/ppermute | solution.py:16
  263.2 11.8 %collective-permute-start.31 = (f32[2,2,8]{2,1,0:T(2,128)S(1)}, f32[2,2,8]{2,1,0:T(2,128)S(1)}, u32[]{:S(2)}, u32[]{:S(2)}) collective-permute-start(f32[2,2,8]{2,1,0:T(2,128)S(1)} %slice.437), channel_id=1, source_target_pairs={{88,0},{96,8},{104,16},{112,24},{120,32},{128,40},{136,48},{144,56... | collective-permute-start | bytes 392 | tf_op jit(solution)/shard_map/ppermute | solution.py:16
  266.9 25.7 %collective-permute-start.28 = (f32[2,5,1]{2,1,0:T(8,128)S(1)}, f32[2,5,1]{2,1,0:T(8,128)S(1)}, u32[]{:S(2)}, u32[]{:S(2)}) collective-permute-start(f32[2,5,1]{2,1,0:T(8,128)S(1)} %get-tuple-element.24), channel_id=1, source_target_pairs={{0,1},{1,2},{2,3},{3,4},{4,5},{5,6},{6,7},{8,9},{9,10},{10,11},{11... | collective-permute-start | bytes 128 | tf_op jit(solution)/shard_map/ppermute | solution.py:24
  272.8 19.8 %collective-permute-start.29 = (f32[2,5,1]{2,1,0:T(8,128)S(1)}, f32[2,5,1]{2,1,0:T(8,128)S(1)}, u32[]{:S(2)}, u32[]{:S(2)}) collective-permute-start(f32[2,5,1]{2,1,0:T(8,128)S(1)} %get-tuple-element.25), channel_id=1, source_target_pairs={{1,0},{2,1},{3,2},{4,3},{5,4},{6,5},{7,6},{9,8},{10,9},{11,10},{12... | collective-permute-start | bytes 128 | tf_op jit(solution)/shard_map/ppermute | solution.py:27
  275.1 17.4 %collective-permute-start.33 = (f32[2,1,8]{2,1,0:T(1,128)S(1)}, f32[2,1,8]{2,1,0:T(1,128)S(1)}, u32[]{:S(2)}, u32[]{:S(2)}) collective-permute-start(f32[2,1,8]{2,1,0:T(1,128)S(1)} %slice.439), channel_id=1, source_target_pairs={{0,80},{8,88},{16,96},{24,104},{32,112},{40,120},{48,128},{56,136}... | collective-permute-start | bytes 200 | tf_op jit(solution)/shard_map/ppermute | solution.py:16
  284.5 8.7 %collective-permute-start.32 = (f32[2,2,8]{2,1,0:T(2,128)S(1)}, f32[2,2,8]{2,1,0:T(2,128)S(1)}, u32[]{:S(2)}, u32[]{:S(2)}) collective-permute-start(f32[2,2,8]{2,1,0:T(2,128)S(1)} %slice.438), channel_id=1, source_target_pairs={{0,88},{8,96},{16,104},{24,112},{32,120},{40,128},{48,136},{56,144... | collective-permute-start | bytes 392 | tf_op jit(solution)/shard_map/ppermute | solution.py:16
  293.4 16.0 %collective-permute-start.38 = (f32[2,1,8]{2,1,0:T(1,128)S(1)}, f32[2,1,8]{2,1,0:T(1,128)S(1)}, u32[]{:S(2)}, u32[]{:S(2)}) collective-permute-start(f32[2,1,8]{2,1,0:T(1,128)S(1)} %get-tuple-element.39), channel_id=1, source_target_pairs={{80,0},{88,8},{96,16},{104,24},{112,32},{120,40},{128,48},{136,56}... | collective-permute-start | bytes 200 | tf_op jit(solution)/shard_map/ppermute | solution.py:16
  297.9 11.8 %collective-permute-start.39 = (f32[2,2,8]{2,1,0:T(2,128)S(1)}, f32[2,2,8]{2,1,0:T(2,128)S(1)}, u32[]{:S(2)}, u32[]{:S(2)}) collective-permute-start(f32[2,2,8]{2,1,0:T(2,128)S(1)} %slice.444), channel_id=1, source_target_pairs={{88,0},{96,8},{104,16},{112,24},{120,32},{128,40},{136,48},{144,56... | collective-permute-start | bytes 392 | tf_op jit(solution)/shard_map/ppermute | solution.py:16
  301.6 25.7 %collective-permute-start.36 = (f32[2,5,1]{2,1,0:T(8,128)S(1)}, f32[2,5,1]{2,1,0:T(8,128)S(1)}, u32[]{:S(2)}, u32[]{:S(2)}) collective-permute-start(f32[2,5,1]{2,1,0:T(8,128)S(1)} %get-tuple-element.22), channel_id=1, source_target_pairs={{0,1},{1,2},{2,3},{3,4},{4,5},{5,6},{6,7},{8,9},{9,10},{10,11},{11... | collective-permute-start | bytes 128 | tf_op jit(solution)/shard_map/ppermute | solution.py:24
  307.5 19.8 %collective-permute-start.37 = (f32[2,5,1]{2,1,0:T(8,128)S(1)}, f32[2,5,1]{2,1,0:T(8,128)S(1)}, u32[]{:S(2)}, u32[]{:S(2)}) collective-permute-start(f32[2,5,1]{2,1,0:T(8,128)S(1)} %get-tuple-element.23), channel_id=1, source_target_pairs={{1,0},{2,1},{3,2},{4,3},{5,4},{6,5},{7,6},{9,8},{10,9},{11,10},{12... | collective-permute-start | bytes 128 | tf_op jit(solution)/shard_map/ppermute | solution.py:27
  309.8 17.4 %collective-permute-start.41 = (f32[2,1,8]{2,1,0:T(1,128)S(1)}, f32[2,1,8]{2,1,0:T(1,128)S(1)}, u32[]{:S(2)}, u32[]{:S(2)}) collective-permute-start(f32[2,1,8]{2,1,0:T(1,128)S(1)} %slice.446), channel_id=1, source_target_pairs={{0,80},{8,88},{16,96},{24,104},{32,112},{40,120},{48,128},{56,136}... | collective-permute-start | bytes 200 | tf_op jit(solution)/shard_map/ppermute | solution.py:16
  319.2 8.7 %collective-permute-start.40 = (f32[2,2,8]{2,1,0:T(2,128)S(1)}, f32[2,2,8]{2,1,0:T(2,128)S(1)}, u32[]{:S(2)}, u32[]{:S(2)}) collective-permute-start(f32[2,2,8]{2,1,0:T(2,128)S(1)} %slice.445), channel_id=1, source_target_pairs={{0,88},{8,96},{16,104},{24,112},{32,120},{40,128},{48,136},{56,144... | collective-permute-start | bytes 392 | tf_op jit(solution)/shard_map/ppermute | solution.py:16
  328.1 16.0 %collective-permute-start.46 = (f32[2,1,8]{2,1,0:T(1,128)S(1)}, f32[2,1,8]{2,1,0:T(1,128)S(1)}, u32[]{:S(2)}, u32[]{:S(2)}) collective-permute-start(f32[2,1,8]{2,1,0:T(1,128)S(1)} %get-tuple-element.37), channel_id=1, source_target_pairs={{80,0},{88,8},{96,16},{104,24},{112,32},{120,40},{128,48},{136,56}... | collective-permute-start | bytes 200 | tf_op jit(solution)/shard_map/ppermute | solution.py:16
  332.6 11.8 %collective-permute-start.47 = (f32[2,2,8]{2,1,0:T(2,128)S(1)}, f32[2,2,8]{2,1,0:T(2,128)S(1)}, u32[]{:S(2)}, u32[]{:S(2)}) collective-permute-start(f32[2,2,8]{2,1,0:T(2,128)S(1)} %slice.451), channel_id=1, source_target_pairs={{88,0},{96,8},{104,16},{112,24},{120,32},{128,40},{136,48},{144,56... | collective-permute-start | bytes 392 | tf_op jit(solution)/shard_map/ppermute | solution.py:16
  336.2 25.7 %collective-permute-start.44 = (f32[2,5,1]{2,1,0:T(8,128)S(1)}, f32[2,5,1]{2,1,0:T(8,128)S(1)}, u32[]{:S(2)}, u32[]{:S(2)}) collective-permute-start(f32[2,5,1]{2,1,0:T(8,128)S(1)} %get-tuple-element.20), channel_id=1, source_target_pairs={{0,1},{1,2},{2,3},{3,4},{4,5},{5,6},{6,7},{8,9},{9,10},{10,11},{11... | collective-permute-start | bytes 128 | tf_op jit(solution)/shard_map/ppermute | solution.py:24
  342.2 19.8 %collective-permute-start.45 = (f32[2,5,1]{2,1,0:T(8,128)S(1)}, f32[2,5,1]{2,1,0:T(8,128)S(1)}, u32[]{:S(2)}, u32[]{:S(2)}) collective-permute-start(f32[2,5,1]{2,1,0:T(8,128)S(1)} %get-tuple-element.21), channel_id=1, source_target_pairs={{1,0},{2,1},{3,2},{4,3},{5,4},{6,5},{7,6},{9,8},{10,9},{11,10},{12... | collective-permute-start | bytes 128 | tf_op jit(solution)/shard_map/ppermute | solution.py:27
  344.5 17.4 %collective-permute-start.49 = (f32[2,1,8]{2,1,0:T(1,128)S(1)}, f32[2,1,8]{2,1,0:T(1,128)S(1)}, u32[]{:S(2)}, u32[]{:S(2)}) collective-permute-start(f32[2,1,8]{2,1,0:T(1,128)S(1)} %slice.453), channel_id=1, source_target_pairs={{0,80},{8,88},{16,96},{24,104},{32,112},{40,120},{48,128},{56,136}... | collective-permute-start | bytes 200 | tf_op jit(solution)/shard_map/ppermute | solution.py:16
  362.7 16.0 %collective-permute-start.54 = (f32[2,1,8]{2,1,0:T(1,128)S(1)}, f32[2,1,8]{2,1,0:T(1,128)S(1)}, u32[]{:S(2)}, u32[]{:S(2)}) collective-permute-start(f32[2,1,8]{2,1,0:T(1,128)S(1)} %get-tuple-element.35), channel_id=1, source_target_pairs={{80,0},{88,8},{96,16},{104,24},{112,32},{120,40},{128,48},{136,56}... | collective-permute-start | bytes 200 | tf_op jit(solution)/shard_map/ppermute | solution.py:16
  367.3 11.8 %collective-permute-start.55 = (f32[2,2,8]{2,1,0:T(2,128)S(1)}, f32[2,2,8]{2,1,0:T(2,128)S(1)}, u32[]{:S(2)}, u32[]{:S(2)}) collective-permute-start(f32[2,2,8]{2,1,0:T(2,128)S(1)} %slice.458), channel_id=1, source_target_pairs={{88,0},{96,8},{104,16},{112,24},{120,32},{128,40},{136,48},{144,56... | collective-permute-start | bytes 392 | tf_op jit(solution)/shard_map/ppermute | solution.py:16
  370.9 25.7 %collective-permute-start.52 = (f32[2,5,1]{2,1,0:T(8,128)S(1)}, f32[2,5,1]{2,1,0:T(8,128)S(1)}, u32[]{:S(2)}, u32[]{:S(2)}) collective-permute-start(f32[2,5,1]{2,1,0:T(8,128)S(1)} %get-tuple-element.18), channel_id=1, source_target_pairs={{0,1},{1,2},{2,3},{3,4},{4,5},{5,6},{6,7},{8,9},{9,10},{10,11},{11... | collective-permute-start | bytes 128 | tf_op jit(solution)/shard_map/ppermute | solution.py:24
  376.8 19.8 %collective-permute-start.53 = (f32[2,5,1]{2,1,0:T(8,128)S(1)}, f32[2,5,1]{2,1,0:T(8,128)S(1)}, u32[]{:S(2)}, u32[]{:S(2)}) collective-permute-start(f32[2,5,1]{2,1,0:T(8,128)S(1)} %get-tuple-element.19), channel_id=1, source_target_pairs={{1,0},{2,1},{3,2},{4,3},{5,4},{6,5},{7,6},{9,8},{10,9},{11,10},{12... | collective-permute-start | bytes 128 | tf_op jit(solution)/shard_map/ppermute | solution.py:27
  379.2 17.4 %collective-permute-start.57 = (f32[2,1,8]{2,1,0:T(1,128)S(1)}, f32[2,1,8]{2,1,0:T(1,128)S(1)}, u32[]{:S(2)}, u32[]{:S(2)}) collective-permute-start(f32[2,1,8]{2,1,0:T(1,128)S(1)} %slice.460), channel_id=1, source_target_pairs={{0,80},{8,88},{16,96},{24,104},{32,112},{40,120},{48,128},{56,136}... | collective-permute-start | bytes 200 | tf_op jit(solution)/shard_map/ppermute | solution.py:16
  388.6 8.7 %collective-permute-start.56 = (f32[2,2,8]{2,1,0:T(2,128)S(1)}, f32[2,2,8]{2,1,0:T(2,128)S(1)}, u32[]{:S(2)}, u32[]{:S(2)}) collective-permute-start(f32[2,2,8]{2,1,0:T(2,128)S(1)} %slice.459), channel_id=1, source_target_pairs={{0,88},{8,96},{16,104},{24,112},{32,120},{40,128},{48,136},{56,144... | collective-permute-start | bytes 392 | tf_op jit(solution)/shard_map/ppermute | solution.py:16
  397.4 16.0 %collective-permute-start.62 = (f32[2,1,8]{2,1,0:T(1,128)S(1)}, f32[2,1,8]{2,1,0:T(1,128)S(1)}, u32[]{:S(2)}, u32[]{:S(2)}) collective-permute-start(f32[2,1,8]{2,1,0:T(1,128)S(1)} %get-tuple-element.33), channel_id=1, source_target_pairs={{80,0},{88,8},{96,16},{104,24},{112,32},{120,40},{128,48},{136,56}... | collective-permute-start | bytes 200 | tf_op jit(solution)/shard_map/ppermute | solution.py:16
  402.0 11.8 %collective-permute-start.63 = (f32[2,2,8]{2,1,0:T(2,128)S(1)}, f32[2,2,8]{2,1,0:T(2,128)S(1)}, u32[]{:S(2)}, u32[]{:S(2)}) collective-permute-start(f32[2,2,8]{2,1,0:T(2,128)S(1)} %slice.465), channel_id=1, source_target_pairs={{88,0},{96,8},{104,16},{112,24},{120,32},{128,40},{136,48},{144,56... | collective-permute-start | bytes 392 | tf_op jit(solution)/shard_map/ppermute | solution.py:16
  405.6 25.7 %collective-permute-start.60 = (f32[2,5,1]{2,1,0:T(8,128)S(1)}, f32[2,5,1]{2,1,0:T(8,128)S(1)}, u32[]{:S(2)}, u32[]{:S(2)}) collective-permute-start(f32[2,5,1]{2,1,0:T(8,128)S(1)} %get-tuple-element.16), channel_id=1, source_target_pairs={{0,1},{1,2},{2,3},{3,4},{4,5},{5,6},{6,7},{8,9},{9,10},{10,11},{11... | collective-permute-start | bytes 128 | tf_op jit(solution)/shard_map/ppermute | solution.py:24
  411.5 19.8 %collective-permute-start.61 = (f32[2,5,1]{2,1,0:T(8,128)S(1)}, f32[2,5,1]{2,1,0:T(8,128)S(1)}, u32[]{:S(2)}, u32[]{:S(2)}) collective-permute-start(f32[2,5,1]{2,1,0:T(8,128)S(1)} %get-tuple-element.17), channel_id=1, source_target_pairs={{1,0},{2,1},{3,2},{4,3},{5,4},{6,5},{7,6},{9,8},{10,9},{11,10},{12... | collective-permute-start | bytes 128 | tf_op jit(solution)/shard_map/ppermute | solution.py:27
  413.8 17.4 %collective-permute-start.65 = (f32[2,1,8]{2,1,0:T(1,128)S(1)}, f32[2,1,8]{2,1,0:T(1,128)S(1)}, u32[]{:S(2)}, u32[]{:S(2)}) collective-permute-start(f32[2,1,8]{2,1,0:T(1,128)S(1)} %slice.467), channel_id=1, source_target_pairs={{0,80},{8,88},{16,96},{24,104},{32,112},{40,120},{48,128},{56,136}... | collective-permute-start | bytes 200 | tf_op jit(solution)/shard_map/ppermute | solution.py:16
  423.2 8.7 %collective-permute-start.64 = (f32[2,2,8]{2,1,0:T(2,128)S(1)}, f32[2,2,8]{2,1,0:T(2,128)S(1)}, u32[]{:S(2)}, u32[]{:S(2)}) collective-permute-start(f32[2,2,8]{2,1,0:T(2,128)S(1)} %slice.466), channel_id=1, source_target_pairs={{0,88},{8,96},{16,104},{24,112},{32,120},{40,128},{48,136},{56,144... | collective-permute-start | bytes 392 | tf_op jit(solution)/shard_map/ppermute | solution.py:16
  (22 other events, 122.4 us)
where the time goes:
time: 440 us; the launch traced here: 433 us
  starting transfers between devices  268 us (61%)
  local copies, waits for them, and re-layouts  99.6 us (23%)
  waiting for transfers between devices  41.1 us (9%)
  matrix products  18.1 us (4%)
  other arithmetic  4.98 us (1%)
    ppermute x34, starting transfers between devices, from_behind(): return lax.ppermute(shard, axis, pairs)  177 us
    gather x1, local copies, waits for them, and re-layouts, flow_of(): picked = jnp.take_along_axis(correlation, row_pick, axis=1)  88.4 us
    ppermute x16, starting transfers between devices, with_halo(): lax.ppermute(lax.slice_in_dim(block, block.shape[dim] - width, None, axis...  63.2 us
    ppermute x16, starting transfers between devices, with_halo(): lax.ppermute(lax.slice_in_dim(block, 0, width, axis=dim), axis, backward)  27.9 us
    ppermute x34, waiting for transfers between devices, from_behind(): return lax.ppermute(shard, axis, pairs)  26 us
    ppermute x16, waiting for transfers between devices, with_halo(): lax.ppermute(lax.slice_in_dim(block, 0, width, axis=dim), axis, backward)  15.1 us
  transfers between devices with their start and end apart: 66, of which 23 were waited for; matrix products, arithmetic and copies ran while one was open for 28% of the time, Pallas kernels for 0%

commit v1 on v0

v1 whole, which is shorter than its diff:
```python
import functools

import jax
import jax.numpy as jnp
from jax import lax
from jax.experimental import pallas as pl
from jax.experimental.pallas import tpu as pltpu
from jax.sharding import PartitionSpec as P

MESH = pl.DeviceIdType.MESH
PATCH = 128
ITERS = 8
TILES = 32
COLS = 8
ROWS = 3
SEC = 32
PAIR_ROWS = 64
HALF = 4
PAD = 16

OWN = tuple(range(-3, 4))
AHEAD = tuple(range(8, 14))
BEHIND = tuple(range(-13, -7))
PEERS = tuple((d, e) for d in OWN + AHEAD + BEHIND for e in (-1, 0, 1) if (d, e) != (0, 0))
SLOT = {peer: i for i, peer in enumerate(PEERS)}
SLOT[(0, 0)] = len(PEERS)

TO_UPPER = ((-11, 0, 1), (-11, 1, 2), (-10, 2, 0))
TO_LOWER = ((11, 1, 0), (11, 2, 1), (10, 0, 2))


def wrap(index, count):
    return lax.rem(index + 2 * count, count)


def kernel(
    peaks, image, out, upper, lower, shifted, sums, message, gathered, field,
    own_sem, send_sem, recv_sem, flow_send, flow_recv,
):
    t = lax.axis_index("tile")
    c = lax.axis_index("col")
    half = HALF * PATCH
    block = ROWS * PATCH

    own_upper = pltpu.make_async_copy(
        image.at[:, pl.ds(0, half)], upper.at[pl.ds(0, block)], own_sem.at[0]
    )
    own_lower = pltpu.make_async_copy(
        image.at[:, pl.ds(half, half)], lower.at[pl.ds(block, block)], own_sem.at[1]
    )
    own_upper.start()
    own_lower.start()

    barrier = pltpu.get_barrier_semaphore()
    for d, e in PEERS:
        pl.semaphore_signal(
            barrier, inc=1, device_id=(wrap(t + d, TILES), wrap(c + e, COLS)), device_id_type=MESH
        )
    pl.semaphore_wait(barrier, len(PEERS))

    def patch_row(buffer, row):
        return buffer.at[pl.ds(row * PATCH, PATCH)]

    sends = []
    for to_upper, to_lower in zip(TO_UPPER, TO_LOWER):
        d, src, dst = to_upper
        sends.append((d, image.at[pl.ds(src * PATCH, PATCH), pl.ds(0, half)], lower, dst))
        d, src, dst = to_lower
        sends.append((d, image.at[pl.ds(src * PATCH, PATCH), pl.ds(half, half)], upper, ROWS + dst))

    def bulk(d, src, buffer, chunk):
        return pltpu.make_async_remote_copy(
            src_ref=src,
            dst_ref=patch_row(buffer, chunk),
            send_sem=send_sem.at[chunk],
            recv_sem=recv_sem.at[chunk],
            device_id=(wrap(t + d, TILES), c),
            device_id_type=MESH,
        )

    def exists(d):
        return t + d >= 0 if d < 0 else t + d < TILES

    for send in sends:

        @pl.when(exists(send[0]))
        def _():
            bulk(*send).start()

    own_upper.wait()
    own_lower.wait()

    def one_pair(chunk, patch, is_lower):
        rows = pl.ds(pl.multiple_of(chunk * PATCH, PATCH), PATCH)
        lanes = pl.ds(patch * PATCH, PATCH)
        pair_row = ROWS * t + chunk - is_lower * (ROWS + SEC)
        py = peaks[0, pair_row, patch + is_lower * HALF]
        px = peaks[1, pair_row, patch + is_lower * HALF]
        later = lower[rows, lanes].astype(jnp.float32)
        later = pltpu.roll(later, lax.rem(PATCH - px, PATCH), 1)
        former = upper[rows, lanes].astype(jnp.float32)
        row = pl.ds(patch * 8 + chunk, 1)
        for b in range(3):
            moved = later if b == 1 else pltpu.roll(later, 1 if b == 0 else PATCH - 1, 1)
            shifted[patch, b, pl.ds(PAD, PATCH)] = moved
            shifted[patch, b, pl.ds(0, PAD)] = moved[PATCH - PAD :]
            shifted[patch, b, pl.ds(PAD + PATCH, PAD)] = moved[:PAD]
        for a in range(3):
            for b in range(3):
                product = former * shifted[patch, b, pl.ds(PAD + py + a - 1, PATCH)]
                sums[3 * a + b, row] = jnp.sum(product, axis=0, keepdims=True)
        sums[9, row] = jnp.full((1, PATCH), py.astype(jnp.float32) * (1.0 / PATCH), jnp.float32)
        sums[10, row] = jnp.full((1, PATCH), px.astype(jnp.float32) * (1.0 / PATCH), jnp.float32)

    def one_chunk(step, carry):
        is_lower = lax.rem(step, 2)
        turn = lax.div(step, 2)
        chunk = jnp.where(is_lower == 1, ROWS + turn, lax.rem(turn + 1, ROWS))
        row = ROWS * t + chunk - is_lower * ROWS
        present = jnp.where(is_lower == 1, row >= SEC, row < PAIR_ROWS)

        @pl.when(present)
        def _():
            buffer = lower
            pltpu.make_async_copy(
                patch_row(buffer, 0), patch_row(buffer, 0), recv_sem.at[chunk]
            ).wait()
            for patch in range(HALF):
                one_pair(chunk, patch, is_lower)

        return carry

    lax.fori_loop(0, 2 * ROWS, one_chunk, 0)

    total = jnp.sum(sums[...], axis=-1, keepdims=True)
    window = [total[i] * (1.0 / PATCH) for i in range(9)]
    least = functools.reduce(jnp.minimum, window)
    weight = [w - least + 0.5 for w in window]
    weight_sum = functools.reduce(jnp.add, weight)
    flow_row = total[9] + (sum(weight[6:9]) - sum(weight[0:3])) / weight_sum
    flow_col = total[10] + (sum(weight[2::3]) - sum(weight[0::3])) / weight_sum
    place = lax.broadcasted_iota(jnp.int32, (8 * HALF, PATCH), 0)
    lane = lax.broadcasted_iota(jnp.int32, (8 * HALF, PATCH), 1)
    chunk = lax.rem(place, 8)
    row = ROWS * t + lax.rem(chunk, ROWS)
    present = ((chunk < ROWS) & (row < PAIR_ROWS)) | (
        (chunk >= ROWS) & (chunk < 2 * ROWS) & (row >= SEC)
    )
    column = COLS * c + lax.div(place, 8) + jnp.where(chunk >= ROWS, HALF, 0)
    spread = jnp.where(
        present & (lane == column),
        flow_row,
        jnp.where(present & (lane == column + PATCH // 2), flow_col, 0.0),
    )
    flows = spread[0:8] + spread[8:16] + spread[16:24] + spread[24:32]
    message[...] = flows
    gathered[SLOT[(0, 0)]] = flows

    copies = [
        pltpu.make_async_remote_copy(
            src_ref=message,
            dst_ref=gathered.at[SLOT[(d, e)]],
            send_sem=flow_send,
            recv_sem=flow_recv,
            device_id=(wrap(t - d, TILES), wrap(c - e, COLS)),
            device_id_type=MESH,
        )
        for d, e in PEERS
    ]
    for copy in copies:
        copy.start()
    field[...] = jnp.zeros_like(field)
    inbox = gathered.at[pl.ds(0, len(PEERS))]
    pltpu.make_async_copy(inbox, inbox, flow_recv).wait()

    for group, (offsets, base) in enumerate(((OWN, 9), (AHEAD, -23), (BEHIND, 41))):
        for d in offsets:
            part = gathered[SLOT[(d, -1)]] + gathered[SLOT[(d, 0)]] + gathered[SLOT[(d, 1)]]
            at = pl.ds(ROWS * d + base, ROWS)
            field[2 * group, at] = part[0:ROWS]
            field[2 * group + 1, at] = part[ROWS : 2 * ROWS]

    size = field.shape[1:]
    flow = [
        field[0] + field[3],
        field[2] + field[5],
        field[4] + field[1],
    ]
    place = lax.broadcasted_iota(jnp.int32, size, 0)
    lane = lax.broadcasted_iota(jnp.int32, size, 1)
    column = lax.rem(lane, PATCH // 2)
    row = lax.rem(ROWS * t - 9 + place + ROWS * TILES, ROWS * TILES)
    in_section = lax.rem(row, SEC)
    up_ok, down_ok = in_section != 0, in_section != SEC - 1
    left_ok, right_ok = column != 0, column != PATCH // 2 - 1
    pair_ok = [lax.rem(row + g * SEC, ROWS * TILES) < PAIR_ROWS for g in range(3)]
    shift = [jnp.zeros(size, jnp.float32) for _ in range(3)]
    for _ in range(ITERS):
        error = [
            jnp.where(pair_ok[g], shift[(g + 1) % 3] - shift[g] - flow[g], 0.0) for g in range(3)
        ]
        after = []
        for g in range(3):
            m = shift[g]
            pull = jnp.where(up_ok, m - pltpu.roll(m, 1, 0), 0.0)
            pull = pull + jnp.where(down_ok, m - pltpu.roll(m, size[0] - 1, 0), 0.0)
            pull = pull + jnp.where(left_ok, m - pltpu.roll(m, 1, 1), 0.0)
            pull = pull + jnp.where(right_ok, m - pltpu.roll(m, PATCH - 1, 1), 0.0)
            after.append(m - 0.12 * (1.0 * pull - error[g] + error[(g + 2) % 3]))
        shift = after
    result = pltpu.roll(shift[0], lax.rem(PATCH - COLS * c, PATCH), 1)
    out[0] = result[9 : 9 + ROWS, 0:COLS]
    out[1] = result[9 : 9 + ROWS, PATCH // 2 : PATCH // 2 + COLS]

    for send in sends:

        @pl.when(exists(send[0]))
        def _():
            bulk(*send).wait_send()

    pltpu.make_async_copy(inbox, inbox, flow_send).wait()


def shards(section_image, peak_offsets):
    half = HALF * PATCH
    return pl.pallas_call(
        kernel,
        out_shape=jax.ShapeDtypeStruct((2, ROWS, COLS), jnp.float32),
        in_specs=[
            pl.BlockSpec(memory_space=pltpu.SMEM),
            pl.BlockSpec(memory_space=pl.ANY),
        ],
        out_specs=pl.BlockSpec(memory_space=pltpu.VMEM),
        scratch_shapes=[
            pltpu.VMEM((2 * ROWS * PATCH, half), jnp.bfloat16),
            pltpu.VMEM((2 * ROWS * PATCH, half), jnp.bfloat16),
            pltpu.VMEM((HALF, 3, PATCH + 2 * PAD, PATCH), jnp.float32),
            pltpu.VMEM((11, 8 * HALF, PATCH), jnp.float32),
            pltpu.VMEM((8, PATCH), jnp.float32),
            pltpu.VMEM((len(PEERS) + 1, 8, PATCH), jnp.float32),
            pltpu.VMEM((6, 24, PATCH), jnp.float32),
            pltpu.SemaphoreType.DMA((2,)),
            pltpu.SemaphoreType.DMA((2 * ROWS,)),
            pltpu.SemaphoreType.DMA((2 * ROWS,)),
            pltpu.SemaphoreType.DMA,
            pltpu.SemaphoreType.DMA,
        ],
        compiler_params=pltpu.CompilerParams(collective_id=0, has_side_effects=True),
        name="flow_and_mesh",
    )(peak_offsets, section_image)


def solution(mesh):
    return jax.shard_map(
        shards,
        mesh=mesh,
        in_specs=(P("tile", "col"), P(None, None, "col")),
        out_specs=P(None, "tile", "col"),
        check_vma=False,
    )
```

time: 440 us -> 58.8 us (0.13); the launches traced: 433 us -> 58.5 us
  starting transfers between devices: 268 us -> 0 us
  local copies, waits for them, and re-layouts: 99.6 us -> 2.67 us
  Pallas kernels: 0 us -> 55.8 us
  waiting for transfers between devices: 41.1 us -> 0 us
  matrix products: 18.1 us -> 0 us
  other arithmetic: 4.98 us -> 0 us
    ppermute x66 -> x0, starting transfers between devices: 268 us -> none  [the longest x34 177 us: from_behind(): return lax.ppermute(shard, axis, pairs)]
    gather x4 -> x0, local copies, waits for them, and re-layouts: 92.2 us -> none  [the longest x1 88.4 us: flow_of(): picked = jnp.take_along_axis(correlation, row_pick, axis=1)]
    pallas_call x0 -> x1, Pallas kernels: none -> 55.8 us  [shards(): pl.pallas_call(kernel, out_shape=jax.ShapeDtypeStruct((2, ROWS, COLS), jn...]
    ppermute x66 -> x0, waiting for transfers between devices: 41.1 us -> none  [the longest x34 26 us: from_behind(): return lax.ppermute(shard, axis, pairs)]
    dot_general x16 -> x0, matrix products: 18.1 us -> none  [the longest x1 2.69 us: correlate(): jnp.einsum('npml,lq->npmq', mixed_imag, sine, preferred_element_type=jnp....]
  transfers between devices with their start and end apart: 66 -> 0, of which waited for: 23 -> 0; matrix products, arithmetic and copies ran while one was open for 28% -> 0% of each run, Pallas kernels for 0% -> 0%
where the time goes in v1:
time: 58.8 us; the launch traced here: 58.5 us
  Pallas kernels  55.8 us (95%)
  local copies, waits for them, and re-layouts  2.67 us (5%)
    pallas_call x1, Pallas kernels, shards(): pl.pallas_call(kernel, out_shape=jax.ShapeDtypeStruct((2, ROWS, COLS), jn...  55.8 us
    unnamed x1, local copies, waits for them, and re-layouts  1.41 us
    pallas_call x1, local copies, waits for them, and re-layouts, shards(): pl.pallas_call(kernel, out_shape=jax.ShapeDtypeStruct((2, ROWS, COLS), jn...  1.25 us

profile of v1, /device:TPU:1, one launch (start us, length us, event | category | flops | bytes accessed | tf_op | source)
XLA Modules:
  0.0 58.5 jit_solution(8528314662176135498)
XLA Ops:
  0.0 1.4 %copy.3.peaks = s32[2,64,8]{2,1,0:T(8,128)} copy(s32[2,64,8]{1,2,0:T(8,128)} %param.3) | data formatting | bytes 8192 | tf_op args[1]
  1.4 55.8 %flow_and_mesh.1 = f32[2,3,8]{2,1,0:T(4,128)} custom-call(s32[2,64,8]{2,1,0:T(8,128)} %copy.3.peaks, bf16[384,1024]{1,0:T(8,128)(2,1)} %image.1), custom_call_target="tpu_custom_call" | custom-call | tf_op jit(solution)/shard_map/flow_and_mesh/pallas_call | solution.py:226
  57.3 1.3 %copy.4 = f32[2,3,8]{2,0,1:T(2,128)} copy(f32[2,3,8]{2,1,0:T(4,128)} %flow_and_mesh.1) | data formatting | bytes 384 | tf_op jit(solution)/shard_map/flow_and_mesh/pallas_call | solution.py:226

commit v2 on v1

v2 whole, which is shorter than its diff:
```python
import functools

import jax
import jax.numpy as jnp
from jax import lax
from jax.experimental import pallas as pl
from jax.experimental.pallas import tpu as pltpu
from jax.sharding import PartitionSpec as P

MESH = pl.DeviceIdType.MESH
PATCH = 128
ITERS = 8
TILES = 32
COLS = 8
ROWS = 3
SEC = 32
PAIR_ROWS = 64
PAD = 16
DUO = 2

SPLIT = (4,) * PAIR_ROWS
WORDS = tuple(sum(SPLIT[8 * w + i] // DUO << 3 * i for i in range(8)) for w in range(8))

OWN = tuple(range(-3, 4))
AHEAD = tuple(range(8, 14))
BEHIND = tuple(range(-13, -7))
GROUPS = (OWN, AHEAD, BEHIND)
PEERS = tuple((d, e) for g in GROUPS for d in g for e in (-1, 0, 1) if (d, e) != (0, 0))
SLOT = {
    (d, e): (e + 1) * 24 + 8 * g + i
    for g, offsets in enumerate(GROUPS)
    for i, d in enumerate(offsets)
    for e in (-1, 0, 1)
}

TO_UPPER = ((0, -11, 1), (1, -11, 2), (2, -10, 0))
TO_LOWER = ((1, 11, 0), (2, 11, 1), (0, 10, 2))

BULK = ((10, 0), (11, 0), (-10, 0), (-11, 0))
SIDES = ((0, 1), (0, -1))
NEXT = ((1, 0), (-1, 0))
ROUNDS = (BULK + SIDES, BULK + SIDES, BULK + SIDES + NEXT, BULK + NEXT, BULK + NEXT)


def wrap(index, count):
    return lax.rem(index + 2 * count, count)


def kernel(
    peaks, image, out, own, other, offsets, shifted, sums, message, gathered, field,
    own_sem, send_sem, recv_sem, flow_send, flow_recv, told,
):
    t = lax.axis_index("tile")
    c = lax.axis_index("col")
    duos = COLS // DUO
    width = DUO * PATCH

    own_copy = pltpu.make_async_copy(image, own, own_sem.at[0])
    own_copy.start()
    peak_copy = pltpu.make_async_copy(peaks, offsets, own_sem.at[1])
    peak_copy.start()

    def split(pair_row):
        word = jnp.int32(WORDS[0])
        for i in range(1, 8):
            word = jnp.where(lax.div(pair_row, 8) == i, jnp.int32(WORDS[i]), word)
        return lax.shift_right_logical(word, 3 * lax.rem(pair_row, 8)) & 7

    def bounds(is_lower, row):
        pair_row = jnp.clip(row - SEC if is_lower else row, 0, PAIR_ROWS - 1)
        if is_lower:
            return jnp.where(row >= SEC, split(pair_row), duos), duos
        return 0, jnp.where(row < PAIR_ROWS, split(pair_row), 0)

    def exists(d):
        return (t + d >= 0) & (t + d < TILES)

    def tell(semaphore, peers):
        count = jnp.int32(0)
        for d, e in peers:
            count += exists(d).astype(jnp.int32)

            @pl.when(exists(d))
            def _():
                pl.semaphore_signal(
                    semaphore, inc=1, device_id=(t + d, wrap(c + e, COLS)), device_id_type=MESH
                )

        pl.semaphore_wait(semaphore, count)

    tell(pltpu.get_barrier_semaphore(), ROUNDS[0])

    def bulk(kind, row, d, row_there, duo):
        lanes = pl.ds(pl.multiple_of(duo * width, width), width)
        place = kind * ROWS + row_there
        return pltpu.make_async_remote_copy(
            src_ref=image.at[pl.ds(row * PATCH, PATCH), lanes],
            dst_ref=other.at[kind, pl.ds(row_there * PATCH, PATCH), lanes],
            send_sem=send_sem.at[place, duo],
            recv_sem=recv_sem.at[place, duo],
            device_id=(t + d, c),
            device_id_type=MESH,
        )

    def sent(kind, row):
        there = ROWS * t + row + (SEC if kind else -SEC)
        low, high = bounds(kind == 1, there)
        if kind:
            return low, jnp.where(there < SEC * 3, high, low)
        return low, jnp.where(there >= 0, high, low)

    def each_send(act):
        for up, low in zip(TO_UPPER, TO_LOWER):
            for kind, (row, d, row_there) in enumerate((up, low)):

                def step(duo, carry, kind=kind, row=row, d=d, row_there=row_there):
                    act(bulk(kind, row, d, row_there, duo))
                    return carry

                lax.fori_loop(*sent(kind, row), step, 0)

    each_send(lambda copy: copy.start())

    for i, peers in enumerate(ROUNDS[1:]):
        tell(told.at[i], peers)

    own_copy.wait()
    peak_copy.wait()

    def one_pair(kind, row, duo, k):
        patch = duo * DUO + k
        place = kind * ROWS + row
        rows = pl.ds(row * PATCH, PATCH)
        lanes = pl.ds(pl.multiple_of(duo * width, width) + k * PATCH, PATCH)
        pair_row = ROWS * t + row - kind * SEC
        py = offsets[0, patch, pair_row]
        px = offsets[1, patch, pair_row]
        mine = own[rows, lanes].astype(jnp.float32)
        theirs = other[kind, rows, lanes].astype(jnp.float32)
        former, later = (theirs, mine) if kind else (mine, theirs)
        later = pltpu.roll(later, lax.rem(PATCH - px, PATCH), 1)
        for b in range(3):
            moved = later if b == 1 else pltpu.roll(later, 1 if b == 0 else PATCH - 1, 1)
            shifted[k, b, pl.ds(PAD, PATCH)] = moved
            shifted[k, b, pl.ds(0, PAD)] = moved[PATCH - PAD :]
            shifted[k, b, pl.ds(PAD + PATCH, PAD)] = moved[:PAD]
        at = pl.ds(patch * 8 + place, 1)
        for a in range(3):
            for b in range(3):
                product = former * shifted[k, b, pl.ds(PAD + py + a - 1, PATCH)]
                sums[3 * a + b, at] = jnp.sum(product, axis=0, keepdims=True)
        sums[9, at] = jnp.full((1, PATCH), py.astype(jnp.float32) * (1.0 / PATCH), jnp.float32)
        sums[10, at] = jnp.full((1, PATCH), px.astype(jnp.float32) * (1.0 / PATCH), jnp.float32)

    for up, low in zip(TO_UPPER, TO_LOWER):
        for kind, (_, _, row) in enumerate((up, low)):

            def step(duo, carry, kind=kind, row=row):
                lanes = pl.ds(pl.multiple_of(duo * width, width), width)
                part = other.at[kind, pl.ds(row * PATCH, PATCH), lanes]
                pltpu.make_async_copy(part, part, recv_sem.at[kind * ROWS + row, duo]).wait()
                for k in range(DUO):
                    one_pair(kind, row, duo, k)
                return carry

            lax.fori_loop(*bounds(kind == 1, ROWS * t + row), step, 0)

    total = jnp.sum(sums[...], axis=-1, keepdims=True)
    window = [total[i] * (1.0 / PATCH) for i in range(9)]
    least = functools.reduce(jnp.minimum, window)
    weight = [w - least + 0.5 for w in window]
    weight_sum = functools.reduce(jnp.add, weight)
    flow_row = total[9] + (sum(weight[6:9]) - sum(weight[0:3])) / weight_sum
    flow_col = total[10] + (sum(weight[2::3]) - sum(weight[0::3])) / weight_sum
    line = lax.broadcasted_iota(jnp.int32, (8 * COLS, PATCH), 0)
    lane = lax.broadcasted_iota(jnp.int32, (8 * COLS, PATCH), 1)
    place = lax.rem(line, 8)
    patch = lax.div(line, 8)
    present = line < 0
    for kind in range(2):
        for row in range(ROWS):
            low, high = bounds(kind == 1, ROWS * t + row)
            present |= (place == kind * ROWS + row) & (patch >= DUO * low) & (patch < DUO * high)
    column = COLS * lax.rem(c + place, COLS) + patch
    half = PATCH // 2
    flows = jnp.where(
        present & (lane == column),
        flow_row,
        jnp.where(present & (lane == column + half), flow_col, 0.0),
    )
    flows = jnp.sum(flows, axis=0, keepdims=True)
    message[...] = flows
    gathered[pl.ds(SLOT[(0, 0)], 1)] = flows

    copies = [
        pltpu.make_async_remote_copy(
            src_ref=message,
            dst_ref=gathered.at[pl.ds(SLOT[(d, e)], 1)],
            send_sem=flow_send,
            recv_sem=flow_recv,
            device_id=(wrap(t - d, TILES), wrap(c - e, COLS)),
            device_id_type=MESH,
        )
        for d, e in PEERS
    ]
    for copy in copies:
        copy.start()
    field[...] = jnp.zeros_like(field)
    each_send(lambda copy: copy.wait_send())
    inbox = gathered.at[pl.ds(0, len(PEERS))]
    pltpu.make_async_copy(inbox, inbox, flow_recv).wait()

    lane = lax.broadcasted_iota(jnp.int32, (24, PATCH), 1)
    in_half = lax.rem(lane, half)
    group = lax.div(in_half, COLS)
    for q in range(2 * ROWS):
        part = jnp.zeros((24, PATCH), jnp.float32)
        for e in (-1, 0, 1):
            part += jnp.where(
                group == lax.rem(c + e + q + COLS, COLS), gathered[pl.ds((e + 1) * 24, 24)], 0.0
            )
        if q:
            near = pltpu.roll(part, PATCH - COLS * q, 1)
            far = pltpu.roll(part, half - COLS * q, 1)
            part = jnp.where(in_half + COLS * q < half, near, far)
        kind, row = divmod(q, ROWS)
        for g, tiles in enumerate(GROUPS):
            field[kind, g, pl.ds(row + g, len(tiles), stride=ROWS)] = part[8 * g : 8 * g + len(tiles)]

    size = field.shape[2:]
    flow = [field[0, g] + field[1, (g + 1) % 3] for g in range(3)]
    line = lax.broadcasted_iota(jnp.int32, size, 0)
    lane = lax.broadcasted_iota(jnp.int32, size, 1)
    column = lax.rem(lane, half)
    row = lax.rem(ROWS * t - 9 + line + ROWS * TILES, ROWS * TILES)
    in_section = lax.rem(row, SEC)
    up_ok, down_ok = in_section != 0, in_section != SEC - 1
    left_ok, right_ok = column != 0, column != half - 1
    pair_ok = [lax.rem(row + g * SEC, ROWS * TILES) < PAIR_ROWS for g in range(3)]
    shift = [jnp.zeros(size, jnp.float32) for _ in range(3)]
    for _ in range(ITERS):
        error = [
            jnp.where(pair_ok[g], shift[(g + 1) % 3] - shift[g] - flow[g], 0.0) for g in range(3)
        ]
        after = []
        for g in range(3):
            m = shift[g]
            pull = jnp.where(up_ok, m - pltpu.roll(m, 1, 0), 0.0)
            pull = pull + jnp.where(down_ok, m - pltpu.roll(m, size[0] - 1, 0), 0.0)
            pull = pull + jnp.where(left_ok, m - pltpu.roll(m, 1, 1), 0.0)
            pull = pull + jnp.where(right_ok, m - pltpu.roll(m, PATCH - 1, 1), 0.0)
            after.append(m - 0.12 * (1.0 * pull - error[g] + error[(g + 2) % 3]))
        shift = after
    result = pltpu.roll(shift[0], lax.rem(PATCH - COLS * c, PATCH), 1)
    for row in range(ROWS):
        out[row, pl.ds(0, 1)] = result[9 + row : 10 + row, 0:COLS]
        out[row, pl.ds(1, 1)] = result[9 + row : 10 + row, half : half + COLS]

    pltpu.make_async_copy(inbox, inbox, flow_send).wait()


def shards(section_image, peak_offsets):
    block = section_image.shape
    places = (2 * ROWS, COLS // DUO)
    result = pl.pallas_call(
        kernel,
        out_shape=jax.ShapeDtypeStruct((ROWS, 2, COLS), jnp.float32),
        in_specs=[pl.BlockSpec(memory_space=pl.ANY)] * 2,
        out_specs=pl.BlockSpec(memory_space=pltpu.VMEM),
        scratch_shapes=[
            pltpu.VMEM(block, jnp.bfloat16),
            pltpu.VMEM((2, *block), jnp.bfloat16),
            pltpu.SMEM((2, COLS, PAIR_ROWS), jnp.int32),
            pltpu.VMEM((DUO, 3, PATCH + 2 * PAD, PATCH), jnp.float32),
            pltpu.VMEM((11, 8 * COLS, PATCH), jnp.float32),
            pltpu.VMEM((1, PATCH), jnp.float32),
            pltpu.VMEM((72, PATCH), jnp.float32),
            pltpu.VMEM((2, 3, 24, PATCH), jnp.float32),
            pltpu.SemaphoreType.DMA((2,)),
            pltpu.SemaphoreType.DMA(places),
            pltpu.SemaphoreType.DMA(places),
            pltpu.SemaphoreType.DMA,
            pltpu.SemaphoreType.DMA,
            pltpu.SemaphoreType.REGULAR((len(ROUNDS) - 1,)),
        ],
        compiler_params=pltpu.CompilerParams(collective_id=0, has_side_effects=True),
        name="flow_and_mesh",
    )(peak_offsets.transpose(0, 2, 1), section_image)
    return result.transpose(1, 0, 2)


def solution(mesh):
    return jax.shard_map(
        shards,
        mesh=mesh,
        in_specs=(P("tile", "col"), P(None, None, "col")),
        out_specs=P(None, "tile", "col"),
        check_vma=False,
    )
```

time: 58.8 us -> 49 us (0.83)
  Pallas kernels: 55.8 us -> 47.7 us
  local copies, waits for them, and re-layouts: 2.67 us -> 1.26 us
    pallas_call x1, Pallas kernels: 55.8 us -> 47.7 us  [shards(): pl.pallas_call(kernel, out_shape=jax.ShapeDtypeStruct((ROWS, 2, COLS), jn...]
    pallas_call x1 -> x0, local copies, waits for them, and re-layouts: 1.25 us -> none  [shards(): pl.pallas_call(kernel, out_shape=jax.ShapeDtypeStruct((2, ROWS, COLS), jn...]
where the time goes in v2:
time: 49 us; the launch traced here: 48.9 us
  Pallas kernels  47.7 us (97%)
  local copies, waits for them, and re-layouts  1.26 us (3%)
    pallas_call x1, Pallas kernels, shards(): pl.pallas_call(kernel, out_shape=jax.ShapeDtypeStruct((ROWS, 2, COLS), jn...  47.7 us
    unnamed x1, local copies, waits for them, and re-layouts  1.26 us

profile of v2, /device:TPU:1, one launch (start us, length us, event | category | flops | bytes accessed | tf_op | source)
XLA Modules:
  0.0 48.9 jit_solution(16180287168500963657)
XLA Ops:
  0.0 47.7 %flow_and_mesh.1 = f32[3,2,8]{2,1,0:T(2,128)} custom-call(s32[2,8,64]{2,1,0:T(8,128)} %bitcast.3, bf16[384,1024]{1,0:T(8,128)(2,1)} %image.1), custom_call_target="tpu_custom_call" | custom-call | tf_op jit(solution)/shard_map/flow_and_mesh/pallas_call | solution.py:265
  47.7 1.3 %copy.4 = f32[2,3,8]{2,0,1:T(2,128)} copy(f32[2,3,8]{2,0,1:T(2,128)} %bitcast.2) | data formatting | bytes 384

commit v3 on v2

--- a/solution.py
+++ b/solution.py
@@ -18,7 +18,12 @@
 PAD = 16
 DUO = 2
 
-SPLIT = (4,) * PAIR_ROWS
+SPLIT = (
+    4, 4, 4, 4, 4, 4, 4, 4, 4, 4, 4, 4, 4, 4, 4, 8,
+    4, 4, 4, 4, 4, 4, 4, 4, 0, 4, 4, 6, 2, 0, 8, 4,
+    4, 2, 8, 6, 0, 4, 4, 8, 4, 4, 4, 4, 4, 4, 4, 4,
+    4, 4, 4, 6, 4, 4, 4, 4, 4, 4, 4, 4, 4, 4, 4, 4,
+)
 WORDS = tuple(sum(SPLIT[8 * w + i] // DUO << 3 * i for i in range(8)) for w in range(8))
 
 OWN = tuple(range(-3, 4))
@@ -33,8 +38,8 @@
     for e in (-1, 0, 1)
 }
 
-TO_UPPER = ((0, -11, 1), (1, -11, 2), (2, -10, 0))
-TO_LOWER = ((1, 11, 0), (2, 11, 1), (0, 10, 2))
+TO_UPPER = ((2, -10, 0), (0, -11, 1), (1, -11, 2))
+TO_LOWER = ((0, 10, 2), (1, 11, 0), (2, 11, 1))
 
 BULK = ((10, 0), (11, 0), (-10, 0), (-11, 0))
 SIDES = ((0, 1), (0, -1))

time: 49 us -> 46.4 us (0.947)
  Pallas kernels: 47.7 us -> 44.9 us
    pallas_call x1, Pallas kernels: 47.7 us -> 44.9 us  [shards(): pl.pallas_call(kernel, out_shape=jax.ShapeDtypeStruct((ROWS, 2, COLS), jn...]
where the time goes in v3:
time: 46.4 us; the launch traced here: 46.2 us
  Pallas kernels  44.9 us (97%)
  local copies, waits for them, and re-layouts  1.26 us (3%)
    pallas_call x1, Pallas kernels, shards(): pl.pallas_call(kernel, out_shape=jax.ShapeDtypeStruct((ROWS, 2, COLS), jn...  44.9 us
    unnamed x1, local copies, waits for them, and re-layouts  1.26 us

profile of v3, /device:TPU:1, one launch (start us, length us, event | category | flops | bytes accessed | tf_op | source)
XLA Modules:
  0.0 46.2 jit_solution(7948737164472720093)
XLA Ops:
  0.0 44.9 %flow_and_mesh.1 = f32[3,2,8]{2,1,0:T(2,128)} custom-call(s32[2,8,64]{2,1,0:T(8,128)} %bitcast.3, bf16[384,1024]{1,0:T(8,128)(2,1)} %image.1), custom_call_target="tpu_custom_call" | custom-call | tf_op jit(solution)/shard_map/flow_and_mesh/pallas_call | solution.py:270
  44.9 1.3 %copy.4 = f32[2,3,8]{2,0,1:T(2,128)} copy(f32[2,3,8]{2,0,1:T(2,128)} %bitcast.2) | data formatting | bytes 384

commit v4 on v3

--- a/solution.py
+++ b/solution.py
@@ -19,10 +19,10 @@
 DUO = 2
 
 SPLIT = (
-    4, 4, 4, 4, 4, 4, 4, 4, 4, 4, 4, 4, 4, 4, 4, 8,
+    4, 4, 4, 4, 4, 4, 4, 4, 4, 4, 6, 4, 4, 4, 4, 8,
     4, 4, 4, 4, 4, 4, 4, 4, 0, 4, 4, 6, 2, 0, 8, 4,
-    4, 2, 8, 6, 0, 4, 4, 8, 4, 4, 4, 4, 4, 4, 4, 4,
-    4, 4, 4, 6, 4, 4, 4, 4, 4, 4, 4, 4, 4, 4, 4, 4,
+    4, 2, 8, 6, 0, 4, 6, 8, 4, 4, 4, 4, 2, 4, 4, 4,
+    4, 4, 2, 4, 4, 4, 4, 2, 4, 4, 4, 4, 4, 4, 2, 4,
 )
 WORDS = tuple(sum(SPLIT[8 * w + i] // DUO << 3 * i for i in range(8)) for w in range(8))
 

time: 46.4 us -> 45.3 us (0.976)
  Pallas kernels: 44.9 us -> 43.9 us
    pallas_call x1, Pallas kernels: 44.9 us -> 43.9 us  [shards(): pl.pallas_call(kernel, out_shape=jax.ShapeDtypeStruct((ROWS, 2, COLS), jn...]
where the time goes in v4:
time: 45.3 us; the launch traced here: 45.2 us
  Pallas kernels  43.9 us (97%)
  local copies, waits for them, and re-layouts  1.26 us (3%)
    pallas_call x1, Pallas kernels, shards(): pl.pallas_call(kernel, out_shape=jax.ShapeDtypeStruct((ROWS, 2, COLS), jn...  43.9 us
    unnamed x1, local copies, waits for them, and re-layouts  1.26 us

profile of v4, /device:TPU:1, one launch (start us, length us, event | category | flops | bytes accessed | tf_op | source)
XLA Modules:
  0.0 45.2 jit_solution(5656053231850849188)
XLA Ops:
  0.0 43.9 %flow_and_mesh.1 = f32[3,2,8]{2,1,0:T(2,128)} custom-call(s32[2,8,64]{2,1,0:T(8,128)} %bitcast.3, bf16[384,1024]{1,0:T(8,128)(2,1)} %image.1), custom_call_target="tpu_custom_call" | custom-call | tf_op jit(solution)/shard_map/flow_and_mesh/pallas_call | solution.py:270
  43.9 1.3 %copy.4 = f32[2,3,8]{2,0,1:T(2,128)} copy(f32[2,3,8]{2,0,1:T(2,128)} %bitcast.2) | data formatting | bytes 384

commit v5 on v4

--- a/solution.py
+++ b/solution.py
@@ -30,7 +30,10 @@
 AHEAD = tuple(range(8, 14))
 BEHIND = tuple(range(-13, -7))
 GROUPS = (OWN, AHEAD, BEHIND)
-PEERS = tuple((d, e) for g in GROUPS for d in g for e in (-1, 0, 1) if (d, e) != (0, 0))
+FAR = tuple((d, e) for d in (-3, 3) for e in (-1, 1))
+PEERS = tuple(
+    (d, e) for g in GROUPS for d in g for e in (-1, 0, 1) if (d, e) not in ((0, 0), *FAR)
+)
 SLOT = {
     (d, e): (e + 1) * 24 + 8 * g + i
     for g, offsets in enumerate(GROUPS)
@@ -93,6 +96,8 @@
 
         pl.semaphore_wait(semaphore, count)
 
+    for peer in FAR:
+        gathered[pl.ds(SLOT[peer], 1)] = jnp.zeros((1, PATCH), jnp.float32)
     tell(pltpu.get_barrier_semaphore(), ROUNDS[0])
 
     def bulk(kind, row, d, row_there, duo):

time: 45.3 us -> 45.3 us (level)
  no operation moved by 1% of the time
where the time goes in v5:
time: 45.3 us; the launch traced here: 45.2 us
  Pallas kernels  43.9 us (97%)
  local copies, waits for them, and re-layouts  1.26 us (3%)
    pallas_call x1, Pallas kernels, shards(): pl.pallas_call(kernel, out_shape=jax.ShapeDtypeStruct((ROWS, 2, COLS), jn...  43.9 us
    unnamed x1, local copies, waits for them, and re-layouts  1.26 us

profile of v5, /device:TPU:1, one launch (start us, length us, event | category | flops | bytes accessed | tf_op | source)
XLA Modules:
  0.0 45.2 jit_solution(10901546765058215673)
XLA Ops:
  0.0 43.9 %flow_and_mesh.1 = f32[3,2,8]{2,1,0:T(2,128)} custom-call(s32[2,8,64]{2,1,0:T(8,128)} %bitcast.3, bf16[384,1024]{1,0:T(8,128)(2,1)} %image.1), custom_call_target="tpu_custom_call" | custom-call | tf_op jit(solution)/shard_map/flow_and_mesh/pallas_call | solution.py:275
  43.9 1.3 %copy.4 = f32[2,3,8]{2,0,1:T(2,128)} copy(f32[2,3,8]{2,0,1:T(2,128)} %bitcast.2) | data formatting | bytes 384
